TPU v7x, 32 devices: a whole 2x2x4 slice. The times are simulated.
32 devices in a mesh: gx: 4 (over z), gy: 2 (over y), gz: 4 (over x, core).
Axes of the slice: x: 2, y: 2, z: 4, core: 2. Of those that a mesh axis runs over, the one named last changes fastest.
Arguments:
- scalar_field: float32 [32, 64, 2048], P('gx', 'gy', 'gz'), may hold values from -6 to 6
- velocity: float32 [3, 32, 64, 2048], P(None, 'gx', 'gy', 'gz'), may hold values from -2.5 to 2.5
- reaction_rate: float32 [32, 64, 2048], P('gx', 'gy', 'gz'), may hold values from 0.3 to 3
- sample_cells: int32 [4, 2, 512], P('gx', 'gy', 'gz'), may hold values from 0 to 255
- weight_in: bfloat16 [3072, 1024], P(('gx', 'gy', 'gz')), may hold values from -0.1875 to 0.1875
- weight_out: bfloat16 [3072, 512], P(('gx', 'gy', 'gz')), may hold values from -0.109375 to 0.109375
Outputs:
- advanced: float32 [32, 64, 2048], P('gx', 'gy', 'gz')
- grad_in: float32 [3072, 1024], P(('gx', 'gy', 'gz'))
- grad_out: float32 [3072, 512], P(('gx', 'gy', 'gz'))
All inputs are finite; a program needn't handle non-finite values.
Results may differ from a plain program's by a relative error of at most 0.0011.
Values may be sent and summed in bfloat16 or wider, within the bound.
A program may use at most 64 MiB of HBM per device.

v0:
```python
import math

import jax
import jax.numpy as jnp
from jax import lax
from jax.sharding import PartitionSpec as P

STEPS = 3


TIME_STEP = 0.15


def padded_2(shard, sides, width):
    for axis, dim in sides:
        size, length = (lax.axis_size(axis), shard.shape[dim])
        up = [(i, (i + 1) % size) for i in range(size)]
        down = [(j, i) for i, j in up]
        last = lax.slice_in_dim(shard, length - width, length, axis=dim)
        first = lax.slice_in_dim(shard, 0, width, axis=dim)
        before = lax.ppermute(last, axis, up)
        after = lax.ppermute(first, axis, down)
        shard = jnp.concatenate([before, shard, after], axis=dim)
    return shard


def update(padded, velocity, reaction_rate):
    center = padded[1:-1, 1:-1, 1:-1]
    x_plus = padded[2:, 1:-1, 1:-1]
    x_minus = padded[:-2, 1:-1, 1:-1]
    y_plus = padded[1:-1, 2:, 1:-1]
    y_minus = padded[1:-1, :-2, 1:-1]
    z_plus = padded[1:-1, 1:-1, 2:]
    z_minus = padded[1:-1, 1:-1, :-2]
    laplace = x_plus + x_minus + (y_plus + y_minus) + (z_plus + z_minus) - 6.0 * center
    advect = (
        velocity[0] * (x_plus - x_minus)
        + velocity[1] * (y_plus - y_minus)
        + velocity[2] * (z_plus - z_minus)
    )
    return center + TIME_STEP * (laplace - 0.5 * advect - reaction_rate * center)


def dsilu(value):
    sig = jax.nn.sigmoid(value)
    return sig * (1.0 + value * (1.0 - sig))


def shards(scalar_field, velocity, reaction_rate, sample_cells, weight_in, weight_out):
    snaps = []
    current = scalar_field
    for step_num in range(STEPS):
        padded = padded_2(current, (("gx", 0), ("gy", 1), ("gz", 2)), 1)
        current = update(padded, velocity, reaction_rate)
        snaps.append(current)
    cells = scalar_field.shape[0] * scalar_field.shape[1]
    pencil = scalar_field.shape[2]
    picks = sample_cells.reshape(-1)

    def pencils(array):
        return jnp.take(array.reshape(cells, pencil), picks, axis=0)

    inputs_bf = jnp.concatenate([pencils(snaps[0]), pencils(snaps[1])], 1).astype(jnp.bfloat16)
    target = pencils(snaps[2])
    count_all = picks.shape[0] * lax.axis_size("gx") * lax.axis_size("gy") * lax.axis_size("gz")
    scale = 1.0 / math.sqrt(count_all)
    contract_last = (((1,), (1,)), ((), ()))
    contract_first = (((0,), (0,)), ((), ()))
    block_in, block_out = (
        lax.all_gather(weight_in, ("gy", "gz"), axis=0, tiled=True),
        lax.all_gather(weight_out, ("gy", "gz"), axis=0, tiled=True),
    )
    all_inputs = lax.all_gather(inputs_bf, "gx", axis=0, tiled=True)
    preact = lax.dot_general(
        all_inputs, block_in, contract_last, preferred_element_type=jnp.float32
    )
    hidden = jax.nn.silu(preact).astype(jnp.bfloat16)
    partial_out = jnp.dot(hidden, block_out, preferred_element_type=jnp.float32)
    predict = lax.psum_scatter(partial_out, "gx", scatter_dimension=0, tiled=True)
    resid = ((predict - target) * scale).astype(jnp.bfloat16)
    all_resid = lax.all_gather(resid, "gx", axis=0, tiled=True)
    back = lax.dot_general(all_resid, block_out, contract_last, preferred_element_type=jnp.float32)
    dpre = (back * dsilu(preact)).astype(jnp.bfloat16)
    part_in = lax.dot_general(dpre, all_inputs, contract_first, preferred_element_type=jnp.float32)
    part_out = lax.dot_general(
        hidden, all_resid, contract_first, preferred_element_type=jnp.float32
    )
    grad_in, grad_out = (
        lax.psum_scatter(part_in, ("gy", "gz"), scatter_dimension=0, tiled=True),
        lax.psum_scatter(part_out, ("gy", "gz"), scatter_dimension=0, tiled=True),
    )
    return (snaps[2], grad_in, grad_out)


def solution(mesh):
    in_specs = (
        P("gx", "gy", "gz"),
        P(None, "gx", "gy", "gz"),
        P("gx", "gy", "gz"),
        P("gx", "gy", "gz"),
        P(("gx", "gy", "gz"), None),
        P(("gx", "gy", "gz"), None),
    )
    out_specs = (P("gx", "gy", "gz"), P(("gx", "gy", "gz"), None), P(("gx", "gy", "gz"), None))
    return jax.shard_map(shards, mesh=mesh, in_specs=in_specs, out_specs=out_specs, check_vma=False)
```

profile of v0, /device:TPU:0, one launch (start us, length us, event | category | flops | bytes accessed | tf_op | source)
XLA Modules:
  0.0 253.4 jit_solution(2958708744548308569)
XLA Ops:
  7.2 1.0 fusion.29
  8.3 3.1 %collective-permute-start.1 = (f32[1,32,512]{2,1,0:T(8,128)S(1)}, f32[1,32,512]{2,1,0:T(8,128)S(1)}, u32[]{:S(2)}, u32[]{:S(2)}) collective-permute-start(f32[1,32,512]{2,1,0:T(8,128)S(1)} %get-tuple-element.21), channel_id=1, source_target_pairs={{0,8},{8,16},{16,24},{24,0},{1,9},{9,17},{17,25},{25,1},{2,10},{10... | collective-permute-start | bytes 196616 | tf_op jit(solution)/shard_map/ppermute | solution.py:21
  11.4 2.1 collective-permute-start
  13.5 2.3 collective-permute-done.1
  15.8 1.1 constant_dynamic-update-slice_fusion.1
  16.9 2.0 collective-permute-start.2
  19.0 1.7 collective-permute-done.2
  20.8 2.0 collective-permute-done.3
  23.4 4.0 %collective-permute-done.4 = f32[10,34,1]{2,1,0:T(8,128)S(1)} collective-permute-done((f32[10,34,1]{2,1,0:T(8,128)S(1)}, f32[10,34,1]{2,1,0:T(8,128)S(1)}, u32[]{:S(2)}, u32[]{:S(2)}) %collective-permute-start.4) | collective-permute-done | bytes 1392 | tf_op jit(solution)/shard_map/ppermute | solution.py:22
  27.4 2.9 %collective-permute-done.5 = f32[10,34,1]{2,1,0:T(8,128)S(1)} collective-permute-done((f32[10,34,1]{2,1,0:T(8,128)S(1)}, f32[10,34,1]{2,1,0:T(8,128)S(1)}, u32[]{:S(2)}, u32[]{:S(2)}) %collective-permute-start.5) | collective-permute-done | bytes 1392 | tf_op jit(solution)/shard_map/ppermute | solution.py:21
  30.3 0.7 fusion.7
  31.1 2.4 collective-permute-start.6
  33.5 2.3 collective-permute-done.6
  35.8 3.8 %collective-permute-done.7 = f32[1,32,512]{2,1,0:T(8,128)S(1)} collective-permute-done((f32[1,32,512]{2,1,0:T(8,128)S(1)}, f32[1,32,512]{2,1,0:T(8,128)S(1)}, u32[]{:S(2)}, u32[]{:S(2)}) %collective-permute-start.7) | collective-permute-done | bytes 65568 | tf_op jit(solution)/shard_map/ppermute | solution.py:21
  39.9 1.8 collective-permute-start.9
  41.7 1.7 collective-permute-done.8
  44.4 0.8 gather_fusion
  45.2 4.1 %collective-permute-done.10 = f32[10,34,1]{2,1,0:T(8,128)} collective-permute-done((f32[10,34,1]{2,1,0:T(8,128)S(1)}, f32[10,34,1]{2,1,0:T(8,128)}, u32[]{:S(2)}, u32[]{:S(2)}) %collective-permute-start.10) | collective-permute-done | bytes 1392 | tf_op jit(solution)/shard_map/ppermute | solution.py:22
  49.3 1.3 collective-permute-done.11
  50.6 1.7 fusion.13
  52.3 0.8 gather_fusion.1
  53.2 0.7 pad_maximum_fusion.46
  54.0 0.7 all-gather.5.cloned.1.call-update
  54.7 11.6 %all_gather.14 = bf16[768,512]{1,0:T(8,128)(2,1)} all-gather(bf16[96,512]{1,0:T(8,128)(2,1)S(1)} %copy-done.8), channel_id=1, replica_groups=mesh['gx'=4,'gy'=2,'gz'=4] {'gy','gz'}, dimensions={0}, use_global_device_ids=true | all-gather | bytes 884736 | tf_op jit(solution)/shard_map/all_gather | solution.py:71
  66.4 14.1 %all-gather.3.cloned.1.call-done = bf16[512,1024]{1,0:T(8,128)(2,1)} async-done(((bf16[128,1024]{1,0:T(8,128)(2,1)}), bf16[512,1024]{1,0:T(8,128)(2,1)}) %all-gather.3.cloned.1.call-update) | async-done | bytes 1048592 | tf_op jit(solution)/shard_map/all_gather | solution.py:73
  80.4 26.9 %all-gather.5.cloned.1.call-done = bf16[768,1024]{1,0:T(8,128)(2,1)} async-done(((bf16[96,1024]{1,0:T(8,128)(2,1)}), bf16[768,1024]{1,0:T(8,128)(2,1)}) %all-gather.5.cloned.1.call-update) | async-done | bytes 1572880 | tf_op jit(solution)/shard_map/all_gather | solution.py:70
  107.3 4.0 %multiply_convert_fusion.1 = (bf16[512,768]{1,0:T(8,128)(2,1)S(1)}, f32[512,768]{1,0:T(8,128)}) fusion(bf16[512,1024]{1,0:T(8,128)(2,1)} %all-gather.3.cloned.1.call-done, bf16[768,1024]{1,0:T(8,128)(2,1)} %all-gather.5.cloned.1.call-done), kind=kOutput, calls=%fused_computation.4 | convolution fusion | flops 807272448 | bytes 4980736 | tf_op jit(solution)/shard_map/dot_general | solution.py:74
  111.3 0.9 copy-done.5
  112.3 1.6 fusion.30
  113.9 3.4 %collective-permute-start.12 = (f32[1,32,512]{2,1,0:T(8,128)S(1)}, f32[1,32,512]{2,1,0:T(8,128)S(1)}, u32[]{:S(2)}, u32[]{:S(2)}) collective-permute-start(f32[1,32,512]{2,1,0:T(8,128)S(1)} %get-tuple-element.17), channel_id=1, source_target_pairs={{8,0},{16,8},{24,16},{0,24},{9,1},{17,9},{25,17},{1,25},{10,2},{18... | collective-permute-start | bytes 196616 | tf_op jit(solution)/shard_map/ppermute | solution.py:22
  117.3 2.5 collective-permute-done.12
  119.8 3.6 %collective-permute-done.13 = f32[1,32,512]{2,1,0:T(8,128)S(1)} collective-permute-done((f32[1,32,512]{2,1,0:T(8,128)S(1)}, f32[1,32,512]{2,1,0:T(8,128)S(1)}, u32[]{:S(2)}, u32[]{:S(2)}) %collective-permute-start.13) | collective-permute-done | bytes 65568 | tf_op jit(solution)/shard_map/ppermute | solution.py:21
  123.5 1.5 collective-permute-start.14
  125.0 0.6 collective-permute-start.15
  125.6 1.8 collective-permute-done.14
  127.3 1.4 collective-permute-done.15
  129.4 4.9 %collective-permute-done.16 = f32[10,34,1]{2,1,0:T(8,128)S(1)} collective-permute-done((f32[10,34,1]{2,1,0:T(8,128)S(1)}, f32[10,34,1]{2,1,0:T(8,128)S(1)}, u32[]{:S(2)}, u32[]{:S(2)}) %collective-permute-start.16) | collective-permute-done | bytes 1392 | tf_op jit(solution)/shard_map/ppermute | solution.py:22
  134.3 1.1 collective-permute-done.17
  135.5 0.7 fusion.19
  136.2 0.8 gather_fusion.2
  136.9 4.4 %reduce-scatter.4.cloned.1.call-done = f32[128,512]{1,0:T(8,128)} async-done(((f32[512,512]{1,0:T(8,128)}), f32[128,512]{1,0:T(8,128)}) %reduce-scatter.4.cloned.1.call-update) | async-done | bytes 262160 | tf_op jit(solution)/shard_map/reduce_scatter | solution.py:79
  141.3 1.1 fusion.24
  142.4 15.5 %all_gather.15 = bf16[512,512]{1,0:T(8,128)(2,1)S(1)} all-gather(bf16[128,512]{1,0:T(8,128)(2,1)S(1)} %fusion.24), channel_id=1, replica_groups=mesh['gx'=4,'gy'=2,'gz'=4] {'gx'}, dimensions={0}, use_global_device_ids=true | all-gather | bytes 655360 | tf_op jit(solution)/shard_map/all_gather | solution.py:81
  157.9 1.8 fusion.31
  159.8 1.1 copy-done.9
  160.9 4.9 %fusion = f32[768,1024]{1,0:T(8,128)} fusion(bf16[512,1024]{1,0:T(8,128)(2,1)S(1)} %copy-done.9, f32[512,768]{1,0:T(8,128)} %get-tuple-element.25, bf16[512,512]{1,0:T(8,128)(2,1)S(1)} %all_gather.15, bf16[768,512]{1,0:T(8,128)(2,1)S(1)} %copy-done.4), kind=kOutput, calls=%fused_computation.6 | convolution fusion | flops 1211498496 | bytes 7077888 | tf_op jit(solution)/shard_map/dot_general | solution.py:84
  165.9 31.1 %reduce-scatter.8.cloned.1.call-done = f32[96,512]{1,0:T(8,128)} async-done(((f32[768,512]{1,0:T(8,128)}), f32[96,512]{1,0:T(8,128)}) %reduce-scatter.8.cloned.1.call-update) | async-done | bytes 196624 | tf_op jit(solution)/shard_map/reduce_scatter | solution.py:90
  197.0 49.9 %reduce-scatter.6.cloned.1.call-done = f32[96,1024]{1,0:T(8,128)} async-done(((f32[768,1024]{1,0:T(8,128)}), f32[96,1024]{1,0:T(8,128)}) %reduce-scatter.6.cloned.1.call-update) | async-done | bytes 393232 | tf_op jit(solution)/shard_map/reduce_scatter | solution.py:89
  (55 shorter events, 3.3 us)
Async XLA Ops:
  7.2 23.2 %copy-start.7 = (f32[8,32,512]{2,1,0:T(8,128)S(1)}, f32[8,32,512]{2,1,0:T(8,128)}, u32[]{:S(2)}) copy-start(f32[8,32,512]{2,1,0:T(8,128)} %param.8) | copy-start | bytes 1572868
  7.2 23.2 %copy-start.2 = (f32[8,32,512]{2,1,0:T(8,128)S(1)}, f32[8,32,512]{2,1,0:T(8,128)}, u32[]{:S(2)}) copy-start(f32[8,32,512]{2,1,0:T(8,128)} %param.10) | copy-start | bytes 1572868
  7.2 23.2 %copy-start = (f32[3,8,32,512]{3,2,1,0:T(8,128)S(1)}, f32[3,8,32,512]{3,2,1,0:T(8,128)}, u32[]{:S(2)}) copy-start(f32[3,8,32,512]{3,2,1,0:T(8,128)} %param.9) | copy-start | bytes 4718596
  7.2 73.2 %all-gather.3.cloned.1.call-start = ((), (), s32[]{:S(2)}) async-start(), calls=%async_computation.3 | async-start | bytes 1310720 | tf_op jit(solution)/shard_map/all_gather | solution.py:73
  8.3 7.5 %collective-permute-start.1 = (f32[1,32,512]{2,1,0:T(8,128)S(1)}, f32[1,32,512]{2,1,0:T(8,128)S(1)}, u32[]{:S(2)}, u32[]{:S(2)}) collective-permute-start(f32[1,32,512]{2,1,0:T(8,128)S(1)} %get-tuple-element.21), channel_id=1, source_target_pairs={{0,8},{8,16},{16,24},{24,0},{1,9},{9,17},{17,25},{25,1},{2,10},{10... | collective-permute-start | bytes 196616 | tf_op jit(solution)/shard_map/ppermute | solution.py:21
  11.4 5.5 %collective-permute-start = (f32[1,32,512]{2,1,0:T(8,128)S(1)}, f32[1,32,512]{2,1,0:T(8,128)S(1)}, u32[]{:S(2)}, u32[]{:S(2)}) collective-permute-start(f32[1,32,512]{2,1,0:T(8,128)S(1)} %get-tuple-element.20), channel_id=1, source_target_pairs={{8,0},{16,8},{24,16},{0,24},{9,1},{17,9},{25,17},{1,25},{10,2},{18... | collective-permute-start | bytes 196616 | tf_op jit(solution)/shard_map/ppermute | solution.py:22
  16.9 3.8 %collective-permute-start.2 = (f32[10,1,512]{2,1,0:T(1,128)S(1)}, f32[10,1,512]{2,1,0:T(1,128)S(1)}, u32[]{:S(2)}, u32[]{:S(2)}) collective-permute-start(f32[10,1,512]{2,1,0:T(1,128)S(1)} %get-tuple-element.15), channel_id=1, source_target_pairs={{4,0},{0,4},{5,1},{1,5},{6,2},{2,6},{7,3},{3,7},{12,8},{8,12},{13,... | collective-permute-start | bytes 61448 | tf_op jit(solution)/shard_map/ppermute | solution.py:22
  18.9 3.8 %collective-permute-start.3 = (f32[10,1,512]{2,1,0:T(1,128)S(1)}, f32[10,1,512]{2,1,0:T(1,128)S(1)}, u32[]{:S(2)}, u32[]{:S(2)}) collective-permute-start(f32[10,1,512]{2,1,0:T(1,128)S(1)} %get-tuple-element.14), channel_id=1, source_target_pairs={{0,4},{4,0},{1,5},{5,1},{2,6},{6,2},{3,7},{7,3},{8,12},{12,8},{9,1... | collective-permute-start | bytes 61448 | tf_op jit(solution)/shard_map/ppermute | solution.py:21
  22.9 4.5 %collective-permute-start.4 = (f32[10,34,1]{2,1,0:T(8,128)S(1)}, f32[10,34,1]{2,1,0:T(8,128)S(1)}, u32[]{:S(2)}, u32[]{:S(2)}) collective-permute-start(f32[10,34,1]{2,1,0:T(8,128)S(1)} %get-tuple-element.9), channel_id=1, source_target_pairs={{1,0},{2,1},{3,2},{0,3},{5,4},{6,5},{7,6},{4,7},{9,8},{10,9},{11,1... | collective-permute-start | bytes 4088 | tf_op jit(solution)/shard_map/ppermute | solution.py:22
  22.9 10.6 %copy-start.10 = (s32[1,1,128]{2,1,0:T(1,128)S(1)}, s32[1,1,128]{2,1,0:T(1,128)}, u32[]{:S(2)}) copy-start(s32[1,1,128]{2,1,0:T(1,128)} %param.11) | copy-start | bytes 1540
  22.9 7.4 %collective-permute-start.5 = (f32[10,34,1]{2,1,0:T(8,128)S(1)}, f32[10,34,1]{2,1,0:T(8,128)S(1)}, u32[]{:S(2)}, u32[]{:S(2)}) collective-permute-start(f32[10,34,1]{2,1,0:T(8,128)S(1)} %get-tuple-element.8), channel_id=1, source_target_pairs={{0,1},{1,2},{2,3},{3,0},{4,5},{5,6},{6,7},{7,4},{8,9},{9,10},{10,1... | collective-permute-start | bytes 4088 | tf_op jit(solution)/shard_map/ppermute | solution.py:21
  31.1 4.8 %collective-permute-start.6 = (f32[1,32,512]{2,1,0:T(8,128)S(1)}, f32[1,32,512]{2,1,0:T(8,128)S(1)}, u32[]{:S(2)}, u32[]{:S(2)}) collective-permute-start(f32[1,32,512]{2,1,0:T(8,128)S(1)} %get-tuple-element.19), channel_id=1, source_target_pairs={{8,0},{16,8},{24,16},{0,24},{9,1},{17,9},{25,17},{1,25},{10,2},{18... | collective-permute-start | bytes 196616 | tf_op jit(solution)/shard_map/ppermute | solution.py:22
  33.5 6.1 %collective-permute-start.7 = (f32[1,32,512]{2,1,0:T(8,128)S(1)}, f32[1,32,512]{2,1,0:T(8,128)S(1)}, u32[]{:S(2)}, u32[]{:S(2)}) collective-permute-start(f32[1,32,512]{2,1,0:T(8,128)S(1)} %get-tuple-element.18), channel_id=1, source_target_pairs={{0,8},{8,16},{16,24},{24,0},{1,9},{9,17},{17,25},{25,1},{2,10},{10... | collective-permute-start | bytes 196616 | tf_op jit(solution)/shard_map/ppermute | solution.py:21
  39.6 3.8 %collective-permute-start.8 = (f32[10,1,512]{2,1,0:T(1,128)S(1)}, f32[10,1,512]{2,1,0:T(1,128)S(1)}, u32[]{:S(2)}, u32[]{:S(2)}) collective-permute-start(f32[10,1,512]{2,1,0:T(1,128)S(1)} %get-tuple-element.13), channel_id=1, source_target_pairs={{4,0},{0,4},{5,1},{1,5},{6,2},{2,6},{7,3},{3,7},{12,8},{8,12},{13,... | collective-permute-start | bytes 61448 | tf_op jit(solution)/shard_map/ppermute | solution.py:22
  39.9 3.8 %collective-permute-start.9 = (f32[10,1,512]{2,1,0:T(1,128)S(1)}, f32[10,1,512]{2,1,0:T(1,128)S(1)}, u32[]{:S(2)}, u32[]{:S(2)}) collective-permute-start(f32[10,1,512]{2,1,0:T(1,128)S(1)} %get-tuple-element.12), channel_id=1, source_target_pairs={{0,4},{4,0},{1,5},{5,1},{2,6},{6,2},{3,7},{7,3},{8,12},{12,8},{9,1... | collective-permute-start | bytes 61448 | tf_op jit(solution)/shard_map/ppermute | solution.py:21
  43.9 5.4 %collective-permute-start.10 = (f32[10,34,1]{2,1,0:T(8,128)S(1)}, f32[10,34,1]{2,1,0:T(8,128)}, u32[]{:S(2)}, u32[]{:S(2)}) collective-permute-start(f32[10,34,1]{2,1,0:T(8,128)S(1)} %get-tuple-element.7), channel_id=1, source_target_pairs={{1,0},{2,1},{3,2},{0,3},{5,4},{6,5},{7,6},{4,7},{9,8},{10,9},{11,1... | collective-permute-start | bytes 4088 | tf_op jit(solution)/shard_map/ppermute | solution.py:22
  43.9 6.7 %collective-permute-start.11 = (f32[10,34,1]{2,1,0:T(8,128)S(1)}, f32[10,34,1]{2,1,0:T(8,128)}, u32[]{:S(2)}, u32[]{:S(2)}) collective-permute-start(f32[10,34,1]{2,1,0:T(8,128)S(1)} %get-tuple-element.6), channel_id=1, source_target_pairs={{0,1},{1,2},{2,3},{3,0},{4,5},{5,6},{6,7},{7,4},{8,9},{9,10},{10,1... | collective-permute-start | bytes 4088 | tf_op jit(solution)/shard_map/ppermute | solution.py:21
  52.3 2.5 copy-start.8
  53.9 53.4 %all-gather.5.cloned.1.call-start = ((), (), s32[]{:S(2)}) async-start(), calls=%async_computation.4 | async-start | bytes 1769472 | tf_op jit(solution)/shard_map/all_gather | solution.py:70
  54.7 86.6 %reduce-scatter.4.cloned.1.call-start = ((), (), s32[]{:S(2)}) async-start(), calls=%async_computation.5 | async-start | bytes 1310720 | tf_op jit(solution)/shard_map/reduce_scatter | solution.py:79
  107.3 5.0 %copy-start.3 = (bf16[768,512]{1,0:T(8,128)(2,1)S(1)}, bf16[768,512]{1,0:T(8,128)(2,1)}, u32[]{:S(2)}) copy-start(bf16[768,512]{1,0:T(8,128)(2,1)} %all_gather.14) | copy-start | bytes 2359300
  111.3 0.9 copy-start.5
  113.9 83.1 %reduce-scatter.8.cloned.1.call-start = ((), (), s32[]{:S(2)}) async-start(), calls=%async_computation.7 | async-start | bytes 1769472 | tf_op jit(solution)/shard_map/reduce_scatter | solution.py:90
  113.9 5.9 %collective-permute-start.12 = (f32[1,32,512]{2,1,0:T(8,128)S(1)}, f32[1,32,512]{2,1,0:T(8,128)S(1)}, u32[]{:S(2)}, u32[]{:S(2)}) collective-permute-start(f32[1,32,512]{2,1,0:T(8,128)S(1)} %get-tuple-element.17), channel_id=1, source_target_pairs={{8,0},{16,8},{24,16},{0,24},{9,1},{17,9},{25,17},{1,25},{10,2},{18... | collective-permute-start | bytes 196616 | tf_op jit(solution)/shard_map/ppermute | solution.py:22
  117.3 6.1 %collective-permute-start.13 = (f32[1,32,512]{2,1,0:T(8,128)S(1)}, f32[1,32,512]{2,1,0:T(8,128)S(1)}, u32[]{:S(2)}, u32[]{:S(2)}) collective-permute-start(f32[1,32,512]{2,1,0:T(8,128)S(1)} %get-tuple-element.16), channel_id=1, source_target_pairs={{0,8},{8,16},{16,24},{24,0},{1,9},{9,17},{17,25},{25,1},{2,10},{10... | collective-permute-start | bytes 196616 | tf_op jit(solution)/shard_map/ppermute | solution.py:21
  123.5 3.8 %collective-permute-start.14 = (f32[10,1,512]{2,1,0:T(1,128)S(1)}, f32[10,1,512]{2,1,0:T(1,128)S(1)}, u32[]{:S(2)}, u32[]{:S(2)}) collective-permute-start(f32[10,1,512]{2,1,0:T(1,128)S(1)} %get-tuple-element.11), channel_id=1, source_target_pairs={{4,0},{0,4},{5,1},{1,5},{6,2},{2,6},{7,3},{3,7},{12,8},{8,12},{13,... | collective-permute-start | bytes 61448 | tf_op jit(solution)/shard_map/ppermute | solution.py:22
  125.0 3.8 %collective-permute-start.15 = (f32[10,1,512]{2,1,0:T(1,128)S(1)}, f32[10,1,512]{2,1,0:T(1,128)S(1)}, u32[]{:S(2)}, u32[]{:S(2)}) collective-permute-start(f32[10,1,512]{2,1,0:T(1,128)S(1)} %get-tuple-element.10), channel_id=1, source_target_pairs={{0,4},{4,0},{1,5},{5,1},{2,6},{6,2},{3,7},{7,3},{8,12},{12,8},{9,1... | collective-permute-start | bytes 61448 | tf_op jit(solution)/shard_map/ppermute | solution.py:21
  128.9 5.4 %collective-permute-start.16 = (f32[10,34,1]{2,1,0:T(8,128)S(1)}, f32[10,34,1]{2,1,0:T(8,128)S(1)}, u32[]{:S(2)}, u32[]{:S(2)}) collective-permute-start(f32[10,34,1]{2,1,0:T(8,128)S(1)} %get-tuple-element.5), channel_id=1, source_target_pairs={{1,0},{2,1},{3,2},{0,3},{5,4},{6,5},{7,6},{4,7},{9,8},{10,9},{11,1... | collective-permute-start | bytes 4088 | tf_op jit(solution)/shard_map/ppermute | solution.py:22
  128.9 6.5 %collective-permute-start.17 = (f32[10,34,1]{2,1,0:T(8,128)S(1)}, f32[10,34,1]{2,1,0:T(8,128)S(1)}, u32[]{:S(2)}, u32[]{:S(2)}) collective-permute-start(f32[10,34,1]{2,1,0:T(8,128)S(1)} %get-tuple-element.4), channel_id=1, source_target_pairs={{0,1},{1,2},{2,3},{3,0},{4,5},{5,6},{6,7},{7,4},{8,9},{9,10},{10,1... | collective-permute-start | bytes 4088 | tf_op jit(solution)/shard_map/ppermute | solution.py:21
  136.1 21.8 %copy-start.1 = (f32[8,32,512]{2,1,0:T(8,128)}, f32[8,32,512]{2,1,0:T(8,128)S(1)}, u32[]{:S(2)}) copy-start(f32[8,32,512]{2,1,0:T(8,128)S(1)} %fusion.19) | copy-start | bytes 1572868
  136.2 21.8 %copy-start.6 = (bf16[512,768]{1,0:T(8,128)(2,1)S(1)}, bf16[512,768]{1,0:T(8,128)(2,1)}, u32[]{:S(2)}) copy-start(bf16[512,768]{1,0:T(8,128)(2,1)} %copy-done.5) | copy-start | bytes 2359300
  157.9 1.9 copy-start.4
  159.7 1.2 copy-start.9
  159.7 87.2 %reduce-scatter.6.cloned.1.call-start = ((), (), s32[]{:S(2)}) async-start(), calls=%async_computation.6 | async-start | bytes 3538944 | tf_op jit(solution)/shard_map/reduce_scatter | solution.py:89
Sparse Core Ops, SparseCore 0:
  54.0 26.3 all-gather.2
  82.3 24.9 all-gather.4
  114.0 27.2 reduce-scatter.3
  159.9 37.0 reduce-scatter.7
  200.8 46.0 reduce-scatter.5
where the time goes:
time: 254 us; the launch traced here: 253 us
  waiting for transfers between devices  169 us (67%)
  blocking collectives  27.2 us (11%)
  starting transfers between devices  19.2 us (8%)
  between operations  14 us (6%)
  matrix products  12.3 us (5%)
  local copies, waits for them, and re-layouts  6.56 us (3%)
  other arithmetic  5.47 us (2%)
    reduce_scatter x1, waiting for transfers between devices, shards(): lax.psum_scatter(part_in, ('gy', 'gz'), scatter_dimension=0, tiled=True)  49.9 us
    reduce_scatter x1, waiting for transfers between devices, shards(): lax.psum_scatter(part_out, ('gy', 'gz'), scatter_dimension=0, tiled=True)  31.1 us
    all_gather x1, waiting for transfers between devices, shards(): lax.all_gather(weight_in, ('gy', 'gz'), axis=0, tiled=True)  26.9 us
    ppermute x9, waiting for transfers between devices, padded_2(): after = lax.ppermute(first, axis, down)  23 us
    ppermute x9, waiting for transfers between devices, padded_2(): before = lax.ppermute(last, axis, up)  18.7 us
    all_gather x1, blocking collectives, shards(): all_resid = lax.all_gather(resid, 'gx', axis=0, tiled=True)  15.5 us
    all_gather x1, waiting for transfers between devices, shards(): all_inputs = lax.all_gather(inputs_bf, 'gx', axis=0, tiled=True)  14.1 us
    ppermute x9, starting transfers between devices, padded_2(): after = lax.ppermute(first, axis, down)  11.9 us
  transfers between devices with their start and end apart: 23, of which 22 were waited for; matrix products, arithmetic and copies ran while one was open for 3% of the time, Pallas kernels for 0%

commit v1 on v0

v1 whole, which is shorter than its diff:
```python
import functools
import math

import jax
import jax.numpy as jnp
from jax import lax
from jax.experimental import pallas as pl
from jax.experimental.pallas import tpu as pltpu
from jax.sharding import PartitionSpec as P

STEPS = 3
TIME_STEP = 0.15
SPLIT = 2
NT = (((1,), (1,)), ((), ()))
TN = (((0,), (0,)), ((), ()))
F32 = jnp.float32
BF16 = jnp.bfloat16


def mm(a, b, dims=None):
    if dims is None:
        return jnp.dot(a, b, preferred_element_type=F32)
    return lax.dot_general(a, b, dims, preferred_element_type=F32)


def dsilu(value):
    sig = 1.0 / (1.0 + jnp.exp(-value))
    return sig * (1.0 + value * (1.0 - sig))


def log2(n):
    bits = n.bit_length() - 1
    assert 1 << bits == n
    return bits


def kernel(
    sizes, scale,
    u_ref, vel_ref, rate_ref, picks_ref, win_ref, wout_ref,
    adv_ref, gin_ref, gout_ref,
    snaps, hx, hy_out, hy, hz, xin, win, wout, pre, hid, part, prv, res, g, rbuf,
    halo_s, halo_r, x_s, x_r, w_s, w_r, p_s, p_r, q_s, q_r, g_s, g_r, loc,
):
    T, NY, NZ = sizes
    D = NY * NZ
    nb, nzb = log2(D), log2(NZ)
    gx, gy, gz = lax.axis_index("gx"), lax.axis_index("gy"), lax.axis_index("gz")
    me = gy * NZ + gz
    mb = [(me // (1 << b)) % 2 for b in range(nb)]
    CX, CY, PEN = adv_ref.shape
    S = picks_ref.shape[1]
    Hc = win_ref.shape[0]
    IN = win_ref.shape[1]
    NS = g.shape[0]
    W = g.shape[3]

    def partner(b):
        if b < nzb:
            return {"gz": gz + (1 - 2 * mb[b]) * (1 << b)}
        return {"gy": gy + (1 - 2 * mb[b]) * (1 << (b - nzb))}

    peers = [{"gx": (gx + k) % T} for k in range(1, T)]
    sides = [
        ({"gx": (gx + 1) % T}, {"gx": (gx + T - 1) % T}),
        ({"gy": (gy + 1) % NY}, {"gy": (gy + NY - 1) % NY}),
        ({"gz": (gz + 1) % NZ}, {"gz": (gz + NZ - 1) % NZ}),
    ]

    def remote(src, dst, ss, rs, dev):
        return pltpu.make_async_remote_copy(
            src_ref=src, dst_ref=dst, send_sem=ss, recv_sem=rs,
            device_id=dev, device_id_type=pl.DeviceIdType.MESH,
        )

    own_in = pltpu.make_async_copy(win_ref, win.at[me], loc.at[0])
    own_out = pltpu.make_async_copy(wout_ref, wout.at[me], loc.at[1])
    first = pltpu.make_async_copy(u_ref, snaps.at[0], loc.at[2])
    own_in.start()
    own_out.start()
    first.start()

    barrier = pltpu.get_barrier_semaphore()
    greet = peers + [partner(b) for b in range(nb)] + list(sides[1]) + list(sides[2])
    for dev in greet:
        pl.semaphore_signal(barrier, inc=1, device_id=dev, device_id_type=pl.DeviceIdType.MESH)
    pl.semaphore_wait(barrier, len(greet))
    first.wait()

    w_bufs = ((win, list(range(nb - 1, -1, -1))), (wout, list(range(1, nb)) + [0]))

    def w_copies(stream, stage):
        buf, order = w_bufs[stream]
        done, cur = order[:stage], order[stage]
        out = []
        for k in range(1 << stage):
            c = sum(mb[b] * (1 << b) for b in range(nb) if b not in done)
            c = c + sum(((k >> j) & 1) * (1 << b) for j, b in enumerate(done))
            theirs = c + (1 - 2 * mb[cur]) * (1 << cur)
            slot = (1 << stage) - 1 + k
            sems = (w_s.at[stream, slot], w_r.at[stream, slot])
            send = remote(buf.at[c], buf.at[c], *sems, partner(cur))
            recv = remote(buf.at[theirs], buf.at[theirs], *sems, partner(cur))
            out.append((send, recv))
        return out

    def w_start(stage):
        for stream in range(2):
            for send, _ in w_copies(stream, stage):
                send.start()

    def w_wait(stage):
        for stream in range(2):
            for _, recv in w_copies(stream, stage):
                recv.wait_recv()

    def halo(step):
        cur = snaps.at[step]
        rows = CX * CY
        faces = [
            (cur.at[pl.ds(rows - CY, CY)], hx.at[step, 0], sides[0][0]),
            (cur.at[pl.ds(0, CY)], hx.at[step, 1], sides[0][1]),
            (hy_out.at[step, 0], hy.at[step, 0], sides[1][0]),
            (hy_out.at[step, 1], hy.at[step, 1], sides[1][1]),
            (cur.at[:, pl.ds(PEN - 128, 128)], hz.at[step, 0], sides[2][0]),
            (cur.at[:, pl.ds(0, 128)], hz.at[step, 1], sides[2][1]),
        ]
        return [
            remote(s, d, halo_s.at[step, i], halo_r.at[step, i], dev)
            for i, (s, d, dev) in enumerate(faces)
        ]

    def halo_start(step):
        copies = halo(step)
        for i in (0, 1, 4, 5):
            copies[i].start()
        for i in range(CX):
            hy_out[step, 0, pl.ds(i, 1), :] = snaps[step, pl.ds(i * CY + CY - 1, 1), :]
            hy_out[step, 1, pl.ds(i, 1), :] = snaps[step, pl.ds(i * CY, 1), :]
        copies[2].start()
        copies[3].start()

    row_id = lax.broadcasted_iota(jnp.int32, (CY, PEN), 0)
    lane_id = lax.broadcasted_iota(jnp.int32, (CY, PEN), 1)

    def advance(step):
        for c in halo(step):
            c.wait_recv()

        def layer(i):
            if i < 0:
                return hx[step, 0]
            if i >= CX:
                return hx[step, 1]
            return snaps[step, pl.ds(i * CY, CY), :]

        for i in range(CX):
            u = layer(i)
            xp, xm = layer(i + 1), layer(i - 1)
            yp = jnp.where(row_id == CY - 1, hy[step, 1, pl.ds(i, 1), :], pltpu.roll(u, CY - 1, 0))
            ym = jnp.where(row_id == 0, hy[step, 0, pl.ds(i, 1), :], pltpu.roll(u, 1, 0))
            zhi = hz[step, 1, pl.ds(i * CY, CY), :][:, 0:1]
            zlo = hz[step, 0, pl.ds(i * CY, CY), :][:, 127:128]
            zp = jnp.where(lane_id == PEN - 1, zhi, pltpu.roll(u, PEN - 1, 1))
            zm = jnp.where(lane_id == 0, zlo, pltpu.roll(u, 1, 1))
            lap = (xp + xm) + (yp + ym) + (zp + zm) - 6.0 * u
            adv = vel_ref[0, i] * (xp - xm) + vel_ref[1, i] * (yp - ym) + vel_ref[2, i] * (zp - zm)
            new = u + TIME_STEP * (lap - 0.5 * adv - rate_ref[i] * u)
            if step == STEPS - 1:
                adv_ref[i] = new
            else:
                snaps[step + 1, pl.ds(i * CY, CY), :] = new

    hot = jnp.where(
        lax.broadcasted_iota(jnp.int32, (CX * CY, S), 0) == picks_ref[...], 1.0, 0.0
    ).astype(BF16)

    def x_copies(half):
        cols = pl.ds(half * PEN, PEN)
        return [
            (
                remote(xin.at[gx, :, cols], xin.at[gx, :, cols], x_s.at[half, k], x_r.at[half, k], dev),
                remote(
                    xin.at[(gx + T - 1 - k) % T, :, cols], xin.at[(gx + T - 1 - k) % T, :, cols],
                    x_s.at[half, k], x_r.at[half, k], dev,
                ),
            )
            for k, dev in enumerate(peers)
        ]

    def x_send(half):
        xin[gx, :, pl.ds(half * PEN, PEN)] = mm(hot, snaps[half + 1].astype(BF16), TN).astype(BF16)
        for send, _ in x_copies(half):
            send.start()

    halo_start(0)
    own_in.wait()
    own_out.wait()
    w_start(0)
    w_stage = 0
    for step in range(STEPS):
        advance(step)
        if step < STEPS - 1:
            halo_start(step + 1)
            x_send(step)
        if w_stage < nb - 1:
            w_wait(w_stage)
            w_stage += 1
            w_start(w_stage)
    snap3 = adv_ref[...].reshape(CX * CY, PEN)
    hi = snap3.astype(BF16)
    rest = snap3 - hi.astype(F32)
    mid = rest.astype(BF16)
    low = (rest - mid.astype(F32)).astype(BF16)
    target = (mm(hot, hi, TN) + mm(hot, mid, TN)) + mm(hot, low, TN)
    while True:
        w_wait(w_stage)
        w_stage += 1
        if w_stage == nb:
            break
        w_start(w_stage)
    for half in range(2):
        for _, recv in x_copies(half):
            recv.wait_recv()

    cb = 4 if D % 4 == 0 else D
    SA = T * S

    @pl.loop(0, D // cb)
    def _(b):
        rows = pl.ds(b * cb, cb)
        v = mm(win[rows].reshape(cb * Hc, IN), xin[...].reshape(SA, IN), NT)
        pre[rows] = v.reshape(cb, Hc, SA)
        hid[rows] = (v / (1.0 + jnp.exp(-v))).astype(BF16).reshape(cb, Hc, SA)

    def predict(t):
        h = hid[:, :, pl.ds(pl.multiple_of(t * S, S), S)].reshape(D * Hc, S)
        return mm(h, wout[...].reshape(D * Hc, PEN), TN)

    p_copies = [
        remote(part.at[k], prv.at[k], p_s.at[k], p_r.at[k], dev) for k, dev in enumerate(peers)
    ]
    for k in range(T - 1):
        part[k] = predict((gx + 1 + k) % T)
        p_copies[k].start()
    total = predict(gx)
    for k in range(T - 1):
        p_copies[k].wait_recv()
        total = total + prv[k]
    res[gx] = ((total - target) * scale).astype(BF16)
    q_copies = []
    for k, dev in enumerate(peers):
        src = (gx + T - 1 - k) % T
        send = remote(res.at[gx], res.at[gx], q_s.at[k], q_r.at[k], dev)
        recv = remote(res.at[src], res.at[src], q_s.at[k], q_r.at[k], dev)
        send.start()
        q_copies.append((send, recv))
    for _, recv in q_copies:
        recv.wait_recv()

    orders = [[0] + list(range(1, nb)), [0] + list(range(nb - 1, 0, -1))]
    offs = [sum(D >> (j + 1) for j in range(s)) for s in range(nb)]

    def g_slot(stage, vals):
        return offs[stage] + sum(v * (1 << j) for j, v in enumerate(vals))

    def g_copy(stream, stage, vals):
        order = orders[stream % 2]
        cur = order[stage]
        c = sum(mb[b] * (1 << b) for b in order[:stage]) + (1 - mb[cur]) * (1 << cur)
        c = c + sum(v * (1 << b) for v, b in zip(vals, order[stage + 1:]))
        slot = g_slot(stage, vals)
        keep = c + (2 * mb[cur] - 1) * (1 << cur)
        copy = remote(
            g.at[stream, c], rbuf.at[stream, slot], g_s.at[stream, slot], g_r.at[stream, slot],
            partner(cur),
        )
        return copy, slot, keep

    def patterns(n):
        return [[(k >> j) & 1 for j in range(n)] for k in range(1 << n)]

    for b in range(D // cb):
        rows = pl.ds(b * cb, cb)
        allres = res[...].reshape(SA, PEN)
        back = mm(wout[rows].reshape(cb * Hc, PEN), allres, NT)
        dpre = (back * dsilu(pre[rows].reshape(cb * Hc, SA))).astype(BF16)
        h = hid[rows].reshape(cb * Hc, SA)
        for stream in range(NS):
            if stream < IN // W:
                x = xin[:, :, pl.ds(stream * W, W)].reshape(SA, W)
                val = mm(dpre, x)
            else:
                val = mm(h, res[:, :, pl.ds(stream * W - IN, W)].reshape(SA, W))
            g[stream, rows] = val.reshape(cb, Hc, W)
            rest_bits = orders[stream % 2][1:]
            for vals in patterns(nb - 1):
                low_c = sum(v * (1 << bb) for v, bb in zip(vals, rest_bits))
                if b * cb <= low_c < (b + 1) * cb:
                    g_copy(stream, 0, vals)[0].start()
    for stage in range(nb):
        for stream in range(NS):
            order = orders[stream % 2]
            n = nb - 1 - stage
            if n == 0:
                copy, slot, keep = g_copy(stream, stage, [])
                copy.wait_recv()
                val = g[stream, keep] + rbuf[stream, slot]
                if stream < IN // W:
                    gin_ref[:, pl.ds(stream * W, W)] = val
                else:
                    gout_ref[:, pl.ds(stream * W - IN, W)] = val
                continue
            nxt = mb[order[stage + 1]]
            for flip in (1, 0):
                bit = 1 - nxt if flip else nxt
                for vals in patterns(n - 1):
                    copy, slot, keep = g_copy(stream, stage, [bit] + vals)
                    copy.wait_recv()
                    g[stream, keep] = g[stream, keep] + rbuf[stream, slot]
                    if flip:
                        g_copy(stream, stage + 1, vals)[0].start()

    for step in range(STEPS):
        for c in halo(step):
            c.wait_send()
    for stream in range(2):
        for stage in range(nb):
            for send, _ in w_copies(stream, stage):
                send.wait_send()
    for half in range(2):
        for send, _ in x_copies(half):
            send.wait_send()
    for k in range(T - 1):
        p_copies[k].wait_send()
        q_copies[k][0].wait_send()
    for stream in range(NS):
        for stage in range(nb):
            for vals in patterns(nb - 1 - stage):
                g_copy(stream, stage, vals)[0].wait_send()


def shards(sizes, scalar_field, velocity, reaction_rate, sample_cells, weight_in, weight_out):
    T, NY, NZ = sizes
    D = NY * NZ
    nb = log2(D)
    CX, CY, PEN = scalar_field.shape
    S = sample_cells.shape[-1]
    Hc, IN = weight_in.shape
    SA = T * S
    W = PEN // SPLIT
    NS = (IN + PEN) // W
    scale = 1.0 / math.sqrt(S * T * D)
    rows = CX * CY
    dma = pltpu.SemaphoreType.DMA
    vmem = pl.BlockSpec(memory_space=pltpu.VMEM)
    return tuple(pl.pallas_call(
        functools.partial(kernel, sizes, scale),
        out_shape=(
            jax.ShapeDtypeStruct((CX, CY, PEN), F32),
            jax.ShapeDtypeStruct((Hc, IN), F32),
            jax.ShapeDtypeStruct((Hc, PEN), F32),
        ),
        in_specs=[vmem] * 6,
        out_specs=(vmem,) * 3,
        scratch_shapes=[
            pltpu.VMEM((STEPS, rows, PEN), F32),
            pltpu.VMEM((STEPS, 2, CY, PEN), F32),
            pltpu.VMEM((STEPS, 2, CX, PEN), F32),
            pltpu.VMEM((STEPS, 2, CX, PEN), F32),
            pltpu.VMEM((STEPS, 2, rows, 128), F32),
            pltpu.VMEM((T, S, IN), BF16),
            pltpu.VMEM((D, Hc, IN), BF16),
            pltpu.VMEM((D, Hc, PEN), BF16),
            pltpu.VMEM((D, Hc, SA), F32),
            pltpu.VMEM((D, Hc, SA), BF16),
            pltpu.VMEM((T - 1, S, PEN), F32),
            pltpu.VMEM((T - 1, S, PEN), F32),
            pltpu.VMEM((T, S, PEN), BF16),
            pltpu.VMEM((NS, D, Hc, W), F32),
            pltpu.VMEM((NS, D - 1, Hc, W), F32),
            dma((STEPS, 6)), dma((STEPS, 6)),
            dma((2, T - 1)), dma((2, T - 1)),
            dma((2, D - 1)), dma((2, D - 1)),
            dma((T - 1,)), dma((T - 1,)),
            dma((T - 1,)), dma((T - 1,)),
            dma((NS, D - 1)), dma((NS, D - 1)),
            dma((3,)),
        ],
        compiler_params=pltpu.CompilerParams(
            collective_id=0, has_side_effects=True, vmem_limit_bytes=60 * 1024 * 1024
        ),
    )(
        scalar_field.reshape(rows, PEN), velocity, reaction_rate,
        sample_cells.reshape(1, S), weight_in, weight_out,
    ))


def solution(mesh):
    sizes = (mesh.shape["gx"], mesh.shape["gy"], mesh.shape["gz"])
    in_specs = (
        P("gx", "gy", "gz"),
        P(None, "gx", "gy", "gz"),
        P("gx", "gy", "gz"),
        P("gx", "gy", "gz"),
        P(("gx", "gy", "gz"), None),
        P(("gx", "gy", "gz"), None),
    )
    out_specs = (P("gx", "gy", "gz"), P(("gx", "gy", "gz"), None), P(("gx", "gy", "gz"), None))
    return jax.shard_map(
        functools.partial(shards, sizes), mesh=mesh, in_specs=in_specs, out_specs=out_specs,
        check_vma=False,
    )
```

time: 254 us -> 116 us (0.46)
  waiting for transfers between devices: 169 us -> 0 us
  Pallas kernels: 0 us -> 111 us
  blocking collectives: 27.2 us -> 0 us
  starting transfers between devices: 19.2 us -> 0 us
  between operations: 14 us -> 0.65 us
  matrix products: 12.3 us -> 0 us
  other arithmetic: 5.47 us -> 0 us
    pallas_call x0 -> x1, Pallas kernels: none -> 111 us  [shards(): pl.pallas_call(functools.partial(kernel, sizes, scale), out_shape=(jax.Sh...]
    reduce_scatter x3 -> x0, waiting for transfers between devices: 85.4 us -> none  [the longest x1 49.9 us: shards(): lax.psum_scatter(part_in, ('gy', 'gz'), scatter_dimension=0, tiled=True)]
    ppermute x18 -> x0, waiting for transfers between devices: 41.6 us -> none  [the longest x9 23 us: padded_2(): after = lax.ppermute(first, axis, down)]
    all_gather x2 -> x0, waiting for transfers between devices: 40.9 us -> none  [the longest x1 26.9 us: shards(): lax.all_gather(weight_in, ('gy', 'gz'), axis=0, tiled=True)]
    all_gather x2 -> x0, blocking collectives: 27.2 us -> none  [the longest x1 15.5 us: shards(): all_resid = lax.all_gather(resid, 'gx', axis=0, tiled=True)]
    ppermute x18 -> x0, starting transfers between devices: 19 us -> none  [the longest x9 11.9 us: padded_2(): after = lax.ppermute(first, axis, down)]
    dot_general x4 -> x0, matrix products: 12.3 us -> none  [the longest x1 4.89 us: shards(): lax.dot_general(dpre, all_inputs, contract_first, preferred_element_type=...]
    add x3 -> x0, other arithmetic: 3.07 us -> none  [update(): center + TIME_STEP * (laplace - 0.5 * advect - reaction_rate * center)]
  transfers between devices with their start and end apart: 23 -> 0, of which waited for: 22 -> 0; matrix products, arithmetic and copies ran while one was open for 3% -> 0% of each run, Pallas kernels for 0% -> 0%
where the time goes in v1:
time: 116 us
  Pallas kernels  111 us (96%)
  local copies, waits for them, and re-layouts  4.35 us (4%)
    pallas_call x1, Pallas kernels, shards(): pl.pallas_call(functools.partial(kernel, sizes, scale), out_shape=(jax.Sh...  111 us
    unnamed x5, local copies, waits for them, and re-layouts  4.35 us

profile of v1, /device:TPU:0, one launch (start us, length us, event | category | flops | bytes accessed | tf_op | source)
XLA Modules:
  0.0 115.7 jit_solution(8780672731975688863)
XLA Ops:
  0.6 110.7 %shard_map.85 = (f32[8,32,512]{2,1,0:T(8,128)}, f32[96,1024]{1,0:T(8,128)}, f32[96,512]{1,0:T(8,128)}) custom-call(f32[256,512]{1,0:T(8,128)} %bitcast.2, f32[3,8,32,512]{3,2,1,0:T(8,128)} %vel_ref.1, f32[8,32,512]{2,1,0:T(8,128)} %rate_ref.1, s32[1,128]{1,0:T(1,128)} %bitcast.3, bf16[96,1024]{1,0:T(8,128)(2,1)} %win_ref.1, bf16[96,512]{1,0:T(8,128)(2,1)} %wout_ref.1), custom_call_target="tpu_custom_call" | custom-call | tf_op jit(solution)/shard_map/pallas_call | solution.py:356
  111.4 0.0 copy-start
  111.4 1.9 %copy.12 = f32[8,32,512]{2,1,0:T(8,128)} copy(f32[8,32,512]{2,1,0:T(8,128)} %get-tuple-element.6) | data formatting | bytes 1048576
  113.3 1.8 %copy.13 = f32[96,1024]{1,0:T(8,128)} copy(f32[96,1024]{1,0:T(8,128)} %get-tuple-element.7) | data formatting | bytes 786432
  115.1 0.0 copy-done
  115.1 0.7 copy.14
Async XLA Ops:
  111.4 3.7 %copy-start = (f32[96,512]{1,0:T(8,128)S(1)}, f32[96,512]{1,0:T(8,128)}, u32[]{:S(2)}) copy-start(f32[96,512]{1,0:T(8,128)} %get-tuple-element.8) | copy-start | bytes 589828

commit v2 on v1

--- a/solution.py
+++ b/solution.py
@@ -174,23 +174,37 @@
         lax.broadcasted_iota(jnp.int32, (CX * CY, S), 0) == picks_ref[...], 1.0, 0.0
     ).astype(BF16)
 
-    def x_copies(half):
+    tb = log2(T)
+    tbits = [(gx // (1 << b)) % 2 for b in range(tb)]
+    x_order = list(range(tb - 1, -1, -1))
+
+    def x_copies(half, stage):
         cols = pl.ds(half * PEN, PEN)
-        return [
-            (
-                remote(xin.at[gx, :, cols], xin.at[gx, :, cols], x_s.at[half, k], x_r.at[half, k], dev),
-                remote(
-                    xin.at[(gx + T - 1 - k) % T, :, cols], xin.at[(gx + T - 1 - k) % T, :, cols],
-                    x_s.at[half, k], x_r.at[half, k], dev,
-                ),
-            )
-            for k, dev in enumerate(peers)
-        ]
+        done, cur = x_order[:stage], x_order[stage]
+        dev = {"gx": gx + (1 - 2 * tbits[cur]) * (1 << cur)}
+        out = []
+        for k in range(1 << stage):
+            c = sum(tbits[b] * (1 << b) for b in range(tb) if b not in done)
+            c = c + sum(((k >> j) & 1) * (1 << b) for j, b in enumerate(done))
+            theirs = c + (1 - 2 * tbits[cur]) * (1 << cur)
+            slot = (1 << stage) - 1 + k
+            sems = (x_s.at[half, slot], x_r.at[half, slot])
+            send = remote(xin.at[c, :, cols], xin.at[c, :, cols], *sems, dev)
+            recv = remote(xin.at[theirs, :, cols], xin.at[theirs, :, cols], *sems, dev)
+            out.append((send, recv))
+        return out
+
+    def x_start(half, stage):
+        for send, _ in x_copies(half, stage):
+            send.start()
+
+    def x_wait(half, stage):
+        for _, recv in x_copies(half, stage):
+            recv.wait_recv()
 
     def x_send(half):
         xin[gx, :, pl.ds(half * PEN, PEN)] = mm(hot, snaps[half + 1].astype(BF16), TN).astype(BF16)
-        for send, _ in x_copies(half):
-            send.start()
+        x_start(half, 0)
 
     halo_start(0)
     own_in.wait()
@@ -202,33 +216,55 @@
         if step < STEPS - 1:
             halo_start(step + 1)
             x_send(step)
+        if step > 0:
+            x_wait(0, step - 1)
+            if step < tb:
+                x_start(0, step)
         if w_stage < nb - 1:
             w_wait(w_stage)
             w_stage += 1
             w_start(w_stage)
+    while True:
+        w_wait(w_stage)
+        w_stage += 1
+        if w_stage == nb:
+            break
+        w_start(w_stage)
+    x_wait(1, 0)
+    if tb > 1:
+        x_start(1, 1)
+    for stage in range(STEPS - 1, tb):
+        x_wait(0, stage)
+        if stage + 1 < tb:
+            x_start(0, stage + 1)
     snap3 = adv_ref[...].reshape(CX * CY, PEN)
     hi = snap3.astype(BF16)
     rest = snap3 - hi.astype(F32)
     mid = rest.astype(BF16)
     low = (rest - mid.astype(F32)).astype(BF16)
     target = (mm(hot, hi, TN) + mm(hot, mid, TN)) + mm(hot, low, TN)
-    while True:
-        w_wait(w_stage)
-        w_stage += 1
-        if w_stage == nb:
-            break
-        w_start(w_stage)
-    for half in range(2):
-        for _, recv in x_copies(half):
-            recv.wait_recv()
 
     cb = 4 if D % 4 == 0 else D
     SA = T * S
+
+    def half_product(rows, half):
+        cols = pl.ds(half * PEN, PEN)
+        return mm(win[rows, :, cols].reshape(cb * Hc, PEN), xin[:, :, cols].reshape(SA, PEN), NT)
 
     @pl.loop(0, D // cb)
     def _(b):
         rows = pl.ds(b * cb, cb)
-        v = mm(win[rows].reshape(cb * Hc, IN), xin[...].reshape(SA, IN), NT)
+        pre[rows] = half_product(rows, 0).reshape(cb, Hc, SA)
+
+    for stage in range(1, tb):
+        x_wait(1, stage)
+        if stage + 1 < tb:
+            x_start(1, stage + 1)
+
+    @pl.loop(0, D // cb)
+    def _(b):
+        rows = pl.ds(b * cb, cb)
+        v = pre[rows].reshape(cb * Hc, SA) + half_product(rows, 1)
         pre[rows] = v.reshape(cb, Hc, SA)
         hid[rows] = (v / (1.0 + jnp.exp(-v))).astype(BF16).reshape(cb, Hc, SA)
 
@@ -236,26 +272,36 @@
         h = hid[:, :, pl.ds(pl.multiple_of(t * S, S), S)].reshape(D * Hc, S)
         return mm(h, wout[...].reshape(D * Hc, PEN), TN)
 
-    p_copies = [
-        remote(part.at[k], prv.at[k], p_s.at[k], p_r.at[k], dev) for k, dev in enumerate(peers)
-    ]
+    HP = PEN // 2
+
+    def p_copy(h, k):
+        return remote(part.at[h, k], prv.at[h, k], p_s.at[h, k], p_r.at[h, k], peers[k])
+
     for k in range(T - 1):
-        part[k] = predict((gx + 1 + k) % T)
-        p_copies[k].start()
-    total = predict(gx)
+        val = predict((gx + 1 + k) % T)
+        for h in range(2):
+            part[h, k] = val[:, h * HP:(h + 1) * HP]
+        p_copy(0, k).start()
     for k in range(T - 1):
-        p_copies[k].wait_recv()
-        total = total + prv[k]
-    res[gx] = ((total - target) * scale).astype(BF16)
-    q_copies = []
-    for k, dev in enumerate(peers):
+        p_copy(1, k).start()
+    total = predict(gx) - target
+
+    def q_copy(h, k):
         src = (gx + T - 1 - k) % T
-        send = remote(res.at[gx], res.at[gx], q_s.at[k], q_r.at[k], dev)
-        recv = remote(res.at[src], res.at[src], q_s.at[k], q_r.at[k], dev)
-        send.start()
-        q_copies.append((send, recv))
-    for _, recv in q_copies:
-        recv.wait_recv()
+        cols = pl.ds(h * HP, HP)
+        sems = (q_s.at[h, k], q_r.at[h, k])
+        send = remote(res.at[gx, :, cols], res.at[gx, :, cols], *sems, peers[k])
+        recv = remote(res.at[src, :, cols], res.at[src, :, cols], *sems, peers[k])
+        return send, recv
+
+    for h in range(2):
+        val = total[:, h * HP:(h + 1) * HP]
+        for k in range(T - 1):
+            p_copy(h, k).wait_recv()
+            val = val + prv[h, k]
+        res[gx, :, pl.ds(h * HP, HP)] = (val * scale).astype(BF16)
+        for k in range(T - 1):
+            q_copy(h, k)[0].start()
 
     orders = [[0] + list(range(1, nb)), [0] + list(range(nb - 1, 0, -1))]
     offs = [sum(D >> (j + 1) for j in range(s)) for s in range(nb)]
@@ -279,46 +325,60 @@
     def patterns(n):
         return [[(k >> j) & 1 for j in range(n)] for k in range(1 << n)]
 
+    NI = IN // W
+
+    def put(stream, b, val):
+        g[stream, pl.ds(b * cb, cb)] = val.reshape(cb, Hc, W)
+        rest_bits = orders[stream % 2][1:]
+        for vals in patterns(nb - 1):
+            low_c = sum(v * (1 << bb) for v, bb in zip(vals, rest_bits))
+            if b * cb <= low_c < (b + 1) * cb:
+                g_copy(stream, 0, vals)[0].start()
+
+    def reduce(stream, stage):
+        order = orders[stream % 2]
+        n = nb - 1 - stage
+        if n == 0:
+            copy, slot, keep = g_copy(stream, stage, [])
+            copy.wait_recv()
+            val = g[stream, keep] + rbuf[stream, slot]
+            if stream < NI:
+                gin_ref[:, pl.ds(stream * W, W)] = val
+            else:
+                gout_ref[:, pl.ds(stream * W - IN, W)] = val
+            return
+        nxt = mb[order[stage + 1]]
+        for flip in (1, 0):
+            bit = 1 - nxt if flip else nxt
+            for vals in patterns(n - 1):
+                copy, slot, keep = g_copy(stream, stage, [bit] + vals)
+                copy.wait_recv()
+                g[stream, keep] = g[stream, keep] + rbuf[stream, slot]
+                if flip:
+                    g_copy(stream, stage + 1, vals)[0].start()
+
+    for h in range(2):
+        for k in range(T - 1):
+            q_copy(h, k)[1].wait_recv()
+        for stream in range(NI, NS):
+            if (stream - NI) * W // HP == h:
+                r = res[:, :, pl.ds(stream * W - IN, W)].reshape(SA, W)
+                for b in range(D // cb):
+                    put(stream, b, mm(hid[pl.ds(b * cb, cb)].reshape(cb * Hc, SA), r))
     for b in range(D // cb):
         rows = pl.ds(b * cb, cb)
-        allres = res[...].reshape(SA, PEN)
-        back = mm(wout[rows].reshape(cb * Hc, PEN), allres, NT)
+        back = mm(wout[rows].reshape(cb * Hc, PEN), res[...].reshape(SA, PEN), NT)
         dpre = (back * dsilu(pre[rows].reshape(cb * Hc, SA))).astype(BF16)
-        h = hid[rows].reshape(cb * Hc, SA)
-        for stream in range(NS):
-            if stream < IN // W:
-                x = xin[:, :, pl.ds(stream * W, W)].reshape(SA, W)
-                val = mm(dpre, x)
-            else:
-                val = mm(h, res[:, :, pl.ds(stream * W - IN, W)].reshape(SA, W))
-            g[stream, rows] = val.reshape(cb, Hc, W)
-            rest_bits = orders[stream % 2][1:]
-            for vals in patterns(nb - 1):
-                low_c = sum(v * (1 << bb) for v, bb in zip(vals, rest_bits))
-                if b * cb <= low_c < (b + 1) * cb:
-                    g_copy(stream, 0, vals)[0].start()
+        if b == 0:
+            for stream in range(NI, NS):
+                reduce(stream, 0)
+        for stream in range(NI):
+            x = xin[:, :, pl.ds(stream * W, W)].reshape(SA, W)
+            put(stream, b, mm(dpre, x))
     for stage in range(nb):
-        for stream in range(NS):
-            order = orders[stream % 2]
-            n = nb - 1 - stage
-            if n == 0:
-                copy, slot, keep = g_copy(stream, stage, [])
-                copy.wait_recv()
-                val = g[stream, keep] + rbuf[stream, slot]
-                if stream < IN // W:
-                    gin_ref[:, pl.ds(stream * W, W)] = val
-                else:
-                    gout_ref[:, pl.ds(stream * W - IN, W)] = val
-                continue
-            nxt = mb[order[stage + 1]]
-            for flip in (1, 0):
-                bit = 1 - nxt if flip else nxt
-                for vals in patterns(n - 1):
-                    copy, slot, keep = g_copy(stream, stage, [bit] + vals)
-                    copy.wait_recv()
-                    g[stream, keep] = g[stream, keep] + rbuf[stream, slot]
-                    if flip:
-                        g_copy(stream, stage + 1, vals)[0].start()
+        for stream in list(range(NI, NS)) + list(range(NI)):
+            if stage > 0 or stream < NI:
+                reduce(stream, stage)
 
     for step in range(STEPS):
         for c in halo(step):
@@ -328,11 +388,12 @@
             for send, _ in w_copies(stream, stage):
                 send.wait_send()
     for half in range(2):
-        for send, _ in x_copies(half):
-            send.wait_send()
-    for k in range(T - 1):
-        p_copies[k].wait_send()
-        q_copies[k][0].wait_send()
+        for stage in range(tb):
+            for send, _ in x_copies(half, stage):
+                send.wait_send()
+        for k in range(T - 1):
+            p_copy(half, k).wait_send()
+            q_copy(half, k)[0].wait_send()
     for stream in range(NS):
         for stage in range(nb):
             for vals in patterns(nb - 1 - stage):
@@ -373,16 +434,16 @@
             pltpu.VMEM((D, Hc, PEN), BF16),
             pltpu.VMEM((D, Hc, SA), F32),
             pltpu.VMEM((D, Hc, SA), BF16),
-            pltpu.VMEM((T - 1, S, PEN), F32),
-            pltpu.VMEM((T - 1, S, PEN), F32),
+            pltpu.VMEM((2, T - 1, S, PEN // 2), F32),
+            pltpu.VMEM((2, T - 1, S, PEN // 2), F32),
             pltpu.VMEM((T, S, PEN), BF16),
             pltpu.VMEM((NS, D, Hc, W), F32),
             pltpu.VMEM((NS, D - 1, Hc, W), F32),
             dma((STEPS, 6)), dma((STEPS, 6)),
             dma((2, T - 1)), dma((2, T - 1)),
             dma((2, D - 1)), dma((2, D - 1)),
-            dma((T - 1,)), dma((T - 1,)),
-            dma((T - 1,)), dma((T - 1,)),
+            dma((2, T - 1)), dma((2, T - 1)),
+            dma((2, T - 1)), dma((2, T - 1)),
             dma((NS, D - 1)), dma((NS, D - 1)),
             dma((3,)),
         ],

time: 116 us -> 110 us (0.948)
  Pallas kernels: 111 us -> 104 us
    pallas_call x1, Pallas kernels: 111 us -> 104 us  [shards(): pl.pallas_call(functools.partial(kernel, sizes, scale), out_shape=(jax.Sh...]
where the time goes in v2:
time: 110 us; the launch traced here: 109 us
  Pallas kernels  104 us (95%)
  local copies, waits for them, and re-layouts  4.35 us (4%)
    pallas_call x1, Pallas kernels, shards(): pl.pallas_call(functools.partial(kernel, sizes, scale), out_shape=(jax.Sh...  104 us
    unnamed x5, local copies, waits for them, and re-layouts  4.35 us

profile of v2, /device:TPU:0, one launch (start us, length us, event | category | flops | bytes accessed | tf_op | source)
XLA Modules:
  0.0 109.4 jit_solution(4299746343425270704)
XLA Ops:
  0.6 104.4 %shard_map.85 = (f32[8,32,512]{2,1,0:T(8,128)}, f32[96,1024]{1,0:T(8,128)}, f32[96,512]{1,0:T(8,128)}) custom-call(f32[256,512]{1,0:T(8,128)} %bitcast.2, f32[3,8,32,512]{3,2,1,0:T(8,128)} %vel_ref.1, f32[8,32,512]{2,1,0:T(8,128)} %rate_ref.1, s32[1,128]{1,0:T(1,128)} %bitcast.3, bf16[96,1024]{1,0:T(8,128)(2,1)} %win_ref.1, bf16[96,512]{1,0:T(8,128)(2,1)} %wout_ref.1), custom_call_target="tpu_custom_call" | custom-call | tf_op jit(solution)/shard_map/pallas_call | solution.py:417
  105.1 0.0 copy-start
  105.1 1.9 %copy.12 = f32[8,32,512]{2,1,0:T(8,128)} copy(f32[8,32,512]{2,1,0:T(8,128)} %get-tuple-element.6) | data formatting | bytes 1048576
  107.0 1.8 %copy.13 = f32[96,1024]{1,0:T(8,128)} copy(f32[96,1024]{1,0:T(8,128)} %get-tuple-element.7) | data formatting | bytes 786432
  108.8 0.0 copy-done
  108.8 0.7 copy.14
Async XLA Ops:
  105.1 3.7 %copy-start = (f32[96,512]{1,0:T(8,128)S(1)}, f32[96,512]{1,0:T(8,128)}, u32[]{:S(2)}) copy-start(f32[96,512]{1,0:T(8,128)} %get-tuple-element.8) | copy-start | bytes 589828
